TPU v7x, 256 devices: a whole 4x4x8 slice. The times are simulated.
256 devices in a mesh: row: 16 (over y, z_hi, core), col: 16 (over x, z_lo).
Axes of the slice: x: 4, y: 4, z: 8 (z_hi: 2, z_lo: 4; z = z_hi * 4 + z_lo), core: 2. Of those that a mesh axis runs over, the one named last changes fastest.
Arguments:
- vectors: bfloat16 [16, 131072], P(None, ('row', 'col')), may hold values from -6 to 6
- tiles: bfloat16 [16, 16, 1024, 4096], P('row', 'col'), may hold values from -0.0625 to 0.0625
- tile_rows: int32 [16, 16, 1024], P('row', 'col'), may hold values from 0 to 127
- tile_cols: int32 [16, 16, 1024], P('row', 'col'), may hold values from 0 to 127
- tile_counts: int32 [16, 16], P('row', 'col'), may hold values from 128 to 1024, as said below
Outputs:
- applied: float32 [16, 131072], P(None, ('row', 'col'))
Inputs may be any that keep to these rules, and one draw needn't show every extreme that they name: `tile_counts`: every cell has 128, 256, 512 or 1024 live slots, and some cell has 1024.
All inputs are finite; a program needn't handle non-finite values.
Results may differ from a plain program's by a relative error of at most 0.0003.
Values may be sent and summed in bfloat16 or wider, within the bound.
A program may use at most 128 MiB of HBM per device.

v0:
```python
import jax
import jax.numpy as jnp
from jax import lax
from jax.sharding import PartitionSpec as P

TILE = 64


def tile_terms(blocks, row_ids, col_ids, is_live, row_set, col_set, row_tiles, col_tiles):
    vec_count = row_set.shape[0]
    slots = blocks.shape[0]
    blocks = jnp.where(is_live[:, None, None], blocks, jnp.zeros((), jnp.bfloat16))
    col_pick = col_set[:, col_ids]
    row_pick = row_set[:, row_ids]
    forward = jnp.einsum(
        "vtj,tij->tvi", col_pick, blocks, preferred_element_type=jnp.float32
    ).reshape(slots, vec_count * TILE)
    transposed = jnp.einsum(
        "vti,tij->tvj", row_pick, blocks, preferred_element_type=jnp.float32
    ).reshape(slots, vec_count * TILE)
    forward_rows = jax.ops.segment_sum(forward, row_ids, num_segments=row_tiles)
    transposed_cols = jax.ops.segment_sum(transposed, col_ids, num_segments=col_tiles)
    return (forward_rows, transposed_cols)


def on_device(vectors, tiles, tile_rows, tile_cols, tile_counts):
    vec_count, entries = vectors.shape
    capacity = tiles.shape[2]
    row_whole = lax.all_gather(vectors, "col", axis=1, tiled=True)
    col_whole = lax.all_gather(vectors, "row", axis=1, tiled=True)
    row_tiles = row_whole.shape[1] // TILE
    col_tiles = col_whole.shape[1] // TILE
    row_set = row_whole.reshape(vec_count, row_tiles, TILE)
    col_set = col_whole.reshape(vec_count, col_tiles, TILE)
    blocks = tiles.reshape(capacity, TILE, TILE)
    row_ids = tile_rows.reshape(capacity)
    col_ids = tile_cols.reshape(capacity)
    live_count = tile_counts.reshape(())
    is_live = jnp.arange(capacity, dtype=jnp.int32) < live_count
    forward_rows, transposed_cols = tile_terms(
        blocks, row_ids, col_ids, is_live, row_set, col_set, row_tiles, col_tiles
    )
    own_tiles = entries // TILE
    forward_mine = lax.psum_scatter(forward_rows, "col", scatter_dimension=0, tiled=True)
    transposed_mine = lax.psum_scatter(transposed_cols, "row", scatter_dimension=0, tiled=True)
    total = forward_mine + transposed_mine
    return total.reshape(own_tiles, vec_count, TILE).transpose(1, 0, 2).reshape(vec_count, entries)


def solution(mesh):
    return jax.shard_map(
        on_device,
        mesh=mesh,
        in_specs=(
            P(None, ("row", "col")),
            P("row", "col", None, None),
            P("row", "col", None),
            P("row", "col", None),
            P("row", "col"),
        ),
        out_specs=P(None, ("row", "col")),
        check_vma=False,
    )
```

profile of v0, /device:TPU:8, one launch (start us, length us, event | category | flops | bytes accessed | tf_op | source)
XLA Modules:
  0.0 308.1 jit_solution(3692660765222738388)
XLA Ops:
  6.5 0.0 reduce-scatter.5.cloned.1.call-start
  6.5 12.0 %copy.14 = bf16[1,1,1024,4096]{2,3,1,0:T(8,128)(2,1)} copy(bf16[1,1,1024,4096]{3,2,1,0:T(8,128)(2,1)} %param.6) | data formatting | bytes 16777216 | tf_op args[1]
  19.2 7.1 %broadcast_select_fusion = bf16[1024,64,64]{0,2,1:T(8,128)(2,1)} fusion(bf16[1024,64,64]{0,2,1:T(8,128)(2,1)} %bitcast.22, pred[1024]{0:T(1024)(128)(4,1)S(1)} %iota_compare_fusion), kind=kLoop, calls=%fused_computation.4 | loop fusion | flops 4194304 | bytes 16778240 | tf_op jit(solution)/shard_map/jit(_where)/select_n | solution.py:12
  26.3 0.0 copy-start
  26.3 0.0 copy-start.2
  26.3 24.0 %copy.15 = bf16[1024,64,64]{2,1,0:T(8,128)(2,1)} copy(bf16[1024,64,64]{0,2,1:T(8,128)(2,1)} %broadcast_select_fusion) | data formatting | bytes 16777216 | tf_op jit(solution)/shard_map/jit(_where)/select_n | solution.py:12
  50.3 0.0 copy-done
  50.3 45.9 %all_gather.7 = bf16[16,8192]{1,0:T(8,128)(2,1)S(1)} all-gather(bf16[16,512]{1,0:T(8,128)(2,1)S(1)} %copy-done), channel_id=1, replica_groups=mesh['row'=16,'col'=16] {'col'}, dimensions={1}, use_global_device_ids=true | all-gather | bytes 278528 | tf_op jit(solution)/shard_map/all_gather | solution.py:29
  96.2 0.5 reshape.93
  96.7 0.3 copy.18
  97.1 0.0 copy-done.2
  97.1 8.5 %gather_fusion.1 = bf16[1024,16,64]{2,1,0:T(8,128)(2,1)} fusion(bf16[16,128,64]{2,0,1:T(8,128)(2,1)S(1)} %copy.18, s32[1024]{0:T(1024)S(1)} %broadcast_clamp_fusion), kind=kCustom, calls=%fused_computation.1 | custom fusion | bytes 4198400 | tf_op jit(solution)/shard_map/gather | solution.py:14
  105.6 11.3 %fusion = f32[1024,16,64]{2,1,0:T(8,128)} fusion(bf16[1024,64,64]{2,1,0:T(8,128)(2,1)} %copy.15, bf16[1024,16,64]{2,1,0:T(8,128)(2,1)} %gather_fusion.1), kind=kOutput, calls=%fused_computation.5 | convolution fusion | flops 134217728 | bytes 14680064 | tf_op jit(solution)/shard_map/vti,tij->tvj/dot_general | solution.py:18
  116.9 6.8 %copy.20 = f32[1024,16,64]{0,2,1:T(8,128)} copy(f32[1024,16,64]{2,1,0:T(8,128)} %fusion) | data formatting | bytes 8388608 | tf_op jit(solution)/shard_map/vti,tij->tvj/dot_general | solution.py:18
  123.7 0.0 copy-start.1
  123.7 5.4 %copy.21 = f32[1024,1024]{1,0:T(8,128)} copy(f32[1024,1024]{0,1:T(8,128)} %bitcast.23) | data formatting | bytes 8388608 | tf_op jit(solution)/shard_map/reshape | solution.py:20
  129.1 0.0 copy-done.1
  129.1 11.1 %scatter_custom_fusion.1 = f32[128,1024]{1,0:T(8,128)} fusion(s32[1024]{0:T(1024)S(1)} %bitcast.28, f32[1024,1024]{1,0:T(8,128)} %copy.21, f32[]{:T(128)} %constant.0.clone.1), kind=kCustom, calls=%fused_computation.9 | custom fusion | flops 1048576 | bytes 524800 | tf_op jit(solution)/shard_map/scatter-add | solution.py:22
  140.2 0.0 reduce-scatter.5.cloned.1.call-update
  140.2 0.0 reduce-scatter.3.cloned.1.call-start
  140.3 29.5 %all_gather.6 = bf16[16,8192]{1,0:T(8,128)(2,1)S(1)} all-gather(bf16[16,512]{1,0:T(8,128)(2,1)S(1)} %copy-done), channel_id=1, replica_groups=mesh['row'=16,'col'=16] {'row'}, dimensions={1}, use_global_device_ids=true | all-gather | bytes 278528 | tf_op jit(solution)/shard_map/all_gather | solution.py:30
  169.7 0.5 reshape.88
  170.3 0.3 copy.13
  170.6 8.5 %gather_fusion = bf16[1024,16,64]{2,1,0:T(8,128)(2,1)} fusion(bf16[16,128,64]{2,0,1:T(8,128)(2,1)S(1)} %copy.13, s32[1024]{0:T(1024)S(1)} %broadcast_clamp_fusion.1), kind=kCustom, calls=%fused_computation | custom fusion | bytes 4198400 | tf_op jit(solution)/shard_map/gather | solution.py:13
  179.1 14.9 %fusion.2 = f32[1024,16,64]{2,1,0:T(8,128)} fusion(bf16[1024,64,64]{2,1,0:T(8,128)(2,1)} %copy.15, bf16[1024,16,64]{2,1,0:T(8,128)(2,1)} %gather_fusion), kind=kOutput, calls=%fused_computation.7 | convolution fusion | flops 134217728 | bytes 14680064 | tf_op jit(solution)/shard_map/vtj,tij->tvi/dot_general | solution.py:15
  194.0 6.8 %copy.16 = f32[1024,16,64]{0,2,1:T(8,128)} copy(f32[1024,16,64]{2,1,0:T(8,128)} %fusion.2) | data formatting | bytes 8388608 | tf_op jit(solution)/shard_map/vtj,tij->tvi/dot_general | solution.py:15
  200.8 5.3 %copy.17 = f32[1024,1024]{1,0:T(8,128)} copy(f32[1024,1024]{0,1:T(8,128)} %bitcast.24) | data formatting | bytes 8388608 | tf_op jit(solution)/shard_map/reshape | solution.py:17
  206.2 11.1 %scatter_custom_fusion = f32[128,1024]{1,0:T(8,128)} fusion(s32[1024]{0:T(1024)S(1)} %bitcast.29, f32[1024,1024]{1,0:T(8,128)} %copy.17, f32[]{:T(128)} %constant.0.clone.1), kind=kCustom, calls=%fused_computation.11 | custom fusion | flops 1048576 | bytes 524800 | tf_op jit(solution)/shard_map/scatter-add | solution.py:21
  217.2 0.0 reduce-scatter.3.cloned.1.call-update
  217.3 0.0 reduce-scatter.5.cloned.1.call-done
  217.3 82.4 %reduce-scatter.3.cloned.1.call-done = f32[8,1024]{1,0:T(8,128)} async-done(((f32[128,1024]{1,0:T(8,128)}), f32[8,1024]{1,0:T(8,128)}) %reduce-scatter.3.cloned.1.call-update) | async-done | bytes 32784 | tf_op jit(solution)/shard_map/reduce_scatter | solution.py:44
  299.7 0.8 add.33
  300.4 0.1 reshape.95
  300.6 0.7 reshape.96
  (6 shorter events, 0.1 us)
Async XLA Ops:
  6.5 210.8 %reduce-scatter.5.cloned.1.call-start = ((), (), s32[]{:S(2)}) async-start(), calls=%async_computation.3 | async-start | bytes 557056 | tf_op jit(solution)/shard_map/reduce_scatter | solution.py:45
  26.3 24.0 %copy-start = (bf16[16,512]{1,0:T(8,128)(2,1)S(1)}, bf16[16,512]{1,0:T(8,128)(2,1)}, u32[]{:S(2)}) copy-start(bf16[16,512]{1,0:T(8,128)(2,1)} %param.5) | copy-start | bytes 49156
  26.3 70.8 %copy-start.2 = (s32[1,1,1024]{2,1,0:T(1,128)S(1)}, s32[1,1,1024]{2,1,0:T(1,128)}, u32[]{:S(2)}) copy-start(s32[1,1,1024]{2,1,0:T(1,128)} %param.7) | copy-start | bytes 12292
  123.7 5.4 %copy-start.1 = (s32[1,1,1024]{2,1,0:T(1,128)S(1)}, s32[1,1,1024]{2,1,0:T(1,128)}, u32[]{:S(2)}) copy-start(s32[1,1,1024]{2,1,0:T(1,128)} %param.8) | copy-start | bytes 12292
  140.2 159.4 %reduce-scatter.3.cloned.1.call-start = ((), (), s32[]{:S(2)}) async-start(), calls=%async_computation.2 | async-start | bytes 557056 | tf_op jit(solution)/shard_map/reduce_scatter | solution.py:44
Sparse Core Ops, SparseCore 0:
  140.3 74.4 reduce-scatter.4
  217.4 82.2 reduce-scatter.2
where the time goes:
time: 309 us; the launch traced here: 308 us
  waiting for transfers between devices  82.4 us (27%)
  local copies, waits for them, and re-layouts  79.8 us (26%)
  blocking collectives  75.4 us (24%)
  other arithmetic  30.1 us (10%)
  matrix products  26.1 us (8%)
  between operations  14.1 us (5%)
    reduce_scatter x1, waiting for transfers between devices, on_device(): lax.psum_scatter(forward_rows, 'col', scatter_dimension=0, tiled=True)  82.4 us
    all_gather x1, blocking collectives, on_device(): row_whole = lax.all_gather(vectors, 'col', axis=1, tiled=True)  45.9 us
    all_gather x1, blocking collectives, on_device(): col_whole = lax.all_gather(vectors, 'row', axis=1, tiled=True)  29.5 us
    select_n x1, local copies, waits for them, and re-layouts, tile_terms(): jnp.where(is_live[:, None, None], blocks, jnp.zeros((), jnp.bfloat16))  24 us
    dot_general x1, matrix products, tile_terms(): jnp.einsum('vtj,tij->tvi', col_pick, blocks, preferred_element_type=jnp.f...  14.9 us
    unnamed x7, local copies, waits for them, and re-layouts  12 us
    dot_general x1, matrix products, tile_terms(): jnp.einsum('vti,tij->tvj', row_pick, blocks, preferred_element_type=jnp.f...  11.3 us
    scatter-add x1, other arithmetic, tile_terms(): jax.ops.segment_sum(transposed, col_ids, num_segments=col_tiles)  11.1 us
  transfers between devices with their start and end apart: 2, of which 1 were waited for; matrix products, arithmetic and copies ran while one was open for 15% of the time, Pallas kernels for 0%

commit v1 on v0

v1 whole, which is shorter than its diff:
```python
import functools

import jax
import jax.numpy as jnp
from jax import lax
from jax.experimental import pallas as pl
from jax.experimental.pallas import tpu as pltpu
from jax.sharding import PartitionSpec as P

MESH = pl.DeviceIdType.MESH


class Place:
    def __init__(self):
        self.a, self.b = lax.axis_index("row"), lax.axis_index("col")
        self.y, self.h, self.k = self.a // 4, (self.a // 2) % 2, self.a % 2
        self.x, self.z = self.b // 4, self.b % 4

    def row(self, dy=0, dh=0, dk=0):
        return ((self.y + dy) % 4) * 4 + ((self.h + dh) % 2) * 2 + (self.k + dk) % 2

    def col(self, dx=0, dz=0):
        return ((self.x + dx) % 4) * 4 + (self.z + dz) % 4

    def meet(self):
        peers = [(self.row(dh=1), self.b), (self.row(dk=1), self.b)]
        peers += [(self.row(dy=d), self.b) for d in (1, 2, 3)]
        peers += [(self.a, self.col(dx=d)) for d in (1, 2, 3)]
        peers += [(self.a, self.col(dz=d)) for d in (1, 2, 3)]
        barrier = pltpu.get_barrier_semaphore()
        for peer in peers:
            pl.semaphore_signal(barrier, inc=1, device_id=peer, device_id_type=MESH)
        pl.semaphore_wait(barrier, len(peers))


class Sends:
    def __init__(self, sems):
        self.sems, self.started = sems, []

    def go(self, src, dst, recv_sem, device):
        copy = pltpu.make_async_remote_copy(
            src_ref=src, dst_ref=dst, send_sem=self.sems.at[len(self.started)],
            recv_sem=recv_sem, device_id=device, device_id_type=MESH)
        copy.start()
        self.started.append(copy)

    def arrived(self, dst, recv_sem, device):
        pltpu.make_async_remote_copy(
            src_ref=dst, dst_ref=dst, send_sem=self.sems.at[0],
            recv_sem=recv_sem, device_id=device, device_id_type=MESH).wait_recv()

    def finish(self):
        for copy in self.started:
            copy.wait_send()


def gather_kernel(vec, row_set, col_set, send_sems, row_sems, col_sems):
    at = Place()
    a, b = at.a, at.b
    sends = Sends(send_sems)
    at.meet()
    mine_r, mine_c = row_set.at[b], col_set.at[a]
    sends.go(vec, mine_c, col_sems.at[a], (at.row(dh=1), b))
    for d in (2, 1, 3):
        sends.go(vec, mine_r, row_sems.at[b], (a, at.col(dz=d)))
    for d in (2, 1, 3):
        sends.go(vec, mine_c, col_sems.at[a], (at.row(dy=d), b))
    for d in (2, 1, 3):
        sends.go(vec, mine_r, row_sems.at[b], (a, at.col(dx=d)))
    sends.go(vec, mine_c, col_sems.at[a], (at.row(dk=1), b))
    row_set[b] = vec[...]
    col_set[a] = vec[...]

    def got_r(j):
        sends.arrived(row_set.at[j], row_sems.at[j], (a, b))

    def got_c(j):
        sends.arrived(col_set.at[j], col_sems.at[j], (a, b))

    for d in (1, 3, 2):
        j = at.col(dz=d)
        got_r(j)
        for e in (2, 1, 3):
            sends.go(row_set.at[j], row_set.at[j], row_sems.at[j], (a, at.col(dx=e)))
    j = at.row(dh=1)
    got_c(j)
    for e in (2, 1, 3):
        sends.go(col_set.at[j], col_set.at[j], col_sems.at[j], (at.row(dy=e), b))
    sends.go(col_set.at[j], col_set.at[j], col_sems.at[j], (at.row(dk=1), b))
    for dh in (0, 1):
        for d in (1, 3, 2):
            j = at.row(dy=d, dh=dh)
            got_c(j)
            sends.go(col_set.at[j], col_set.at[j], col_sems.at[j], (at.row(dk=1), b))
    for dh in (0, 1):
        for d in (0, 1, 2, 3):
            got_c(at.row(dy=d, dh=dh, dk=1))
    for d in (1, 3, 2):
        for e in (0, 1, 3, 2):
            got_r(at.col(dx=d, dz=e))
    sends.finish()


def gather(vectors):
    whole = jax.ShapeDtypeStruct((16,) + vectors.shape, vectors.dtype)
    vmem = pl.BlockSpec(memory_space=pltpu.VMEM)
    return pl.pallas_call(
        gather_kernel,
        out_shape=(whole, whole),
        in_specs=[vmem],
        out_specs=(vmem, vmem),
        scratch_shapes=[
            pltpu.SemaphoreType.DMA((30,)),
            pltpu.SemaphoreType.DMA((16,)),
            pltpu.SemaphoreType.DMA((16,)),
        ],
        compiler_params=pltpu.CompilerParams(collective_id=0, has_side_effects=True),
        name="gather",
    )(vectors)


def scatter_kernel(f, c, out, fx, fs, fz, cc, cs, cy, ch, send_sems, fx_sems, fz_sems, cc_sems, cy_sems, ch_sem):
    at = Place()
    a, b = at.a, at.b
    sends = Sends(send_sems)
    at.meet()
    far = (2, 1, 3)
    for dy in (2, 1, 3, 0):
        for dh in (1, 0):
            n = dy * 2 + dh
            sends.go(c.at[at.row(dy=dy, dh=dh, dk=1)], cc.at[n], cc_sems.at[n], (at.row(dk=1), b))
    for dz in (2, 1, 3, 0):
        for dx in far:
            n = dz * 3 + dx - 1
            sends.go(f.at[at.col(dx=dx, dz=dz)], fx.at[n], fx_sems.at[n], (a, at.col(dx=dx)))

    def sum_core(dy, dh):
        n = dy * 2 + dh
        sends.arrived(cc.at[n], cc_sems.at[n], (a, b))
        cs[n] = c[at.row(dy=dy, dh=dh)] + cc[n]

    def sum_x(dz):
        for dx in far:
            n = dz * 3 + dx - 1
            sends.arrived(fx.at[n], fx_sems.at[n], (a, b))
        fs[dz] = (f[at.col(dz=dz)] + fx[dz * 3]) + (fx[dz * 3 + 1] + fx[dz * 3 + 2])

    def sum_y(dh):
        for dy in far:
            n = (dy - 1) * 2 + dh
            sends.arrived(cy.at[n], cy_sems.at[n], (a, b))
        cs[dh] = (cs[dh] + cy[dh]) + (cy[2 + dh] + cy[4 + dh])

    for dy in far:
        for dh in (1, 0):
            sum_core(dy, dh)
            n = (dy - 1) * 2 + dh
            sends.go(cs.at[dy * 2 + dh], cy.at[n], cy_sems.at[n], (at.row(dy=dy), b))
    sum_core(0, 1)
    sum_core(0, 0)
    for dz in far:
        sum_x(dz)
        sends.go(fs.at[dz], fz.at[dz - 1], fz_sems.at[dz - 1], (a, at.col(dz=dz)))
        if dz == 2:
            sum_y(1)
            sends.go(cs.at[1], ch, ch_sem, (at.row(dh=1), b))
    sum_y(0)
    sum_x(0)
    sends.arrived(ch, ch_sem, (a, b))
    total = fs[0] + (cs[0] + ch[...])
    for dz in (1, 3, 2):
        sends.arrived(fz.at[dz - 1], fz_sems.at[dz - 1], (a, b))
    out[...] = total + (fz[0] + (fz[1] + fz[2]))
    sends.finish()


def scatter(f, c):
    block = f.shape[1:]
    vmem = pl.BlockSpec(memory_space=pltpu.VMEM)

    def room(n):
        return pltpu.VMEM((n,) + block, jnp.float32)

    return pl.pallas_call(
        scatter_kernel,
        out_shape=jax.ShapeDtypeStruct(block, jnp.float32),
        in_specs=[vmem, vmem],
        out_specs=vmem,
        scratch_shapes=[
            room(12), room(4), room(3), room(8), room(8), room(6), pltpu.VMEM(block, jnp.float32),
            pltpu.SemaphoreType.DMA((30,)),
            pltpu.SemaphoreType.DMA((12,)),
            pltpu.SemaphoreType.DMA((3,)),
            pltpu.SemaphoreType.DMA((8,)),
            pltpu.SemaphoreType.DMA((6,)),
            pltpu.SemaphoreType.DMA,
        ],
        compiler_params=pltpu.CompilerParams(collective_id=1, has_side_effects=True),
        name="scatter",
    )(f, c)


def lane_low(shape):
    return lax.broadcasted_iota(jnp.int32, shape, 1) < 64

def halves(v):
    lo, hi = v[:, :64], v[:, 64:]
    return jnp.concatenate([lo, lo], axis=1), jnp.concatenate([hi, hi], axis=1)

def local_kernel(copies, rows, cols, count, row_set, col_set, tiles, f_out, c_out, *scratch):
    tbuf, tsem, x2r, x2c = scratch[:4]
    stages = scratch[4:6]
    f_acc = scratch[6:6 + 2 * copies]
    c_acc = scratch[6 + 2 * copies:6 + 4 * copies]
    chunks = count[0] // 32

    def fetch(k):
        at = pl.ds(pl.multiple_of(k * 32, 32), 32)
        return pltpu.make_async_copy(tiles.at[at, :], tbuf.at[at, :], tsem.at[k])

    @pl.loop(0, chunks)
    def _(k):
        fetch(k).start()

    @pl.loop(0, 128)
    def _(r):
        for acc in f_acc + c_acc:
            acc[r] = jnp.zeros((16, 128), jnp.float32)

    @pl.loop(0, 16)
    def _(b):
        for src, dst in ((row_set, x2r), (col_set, x2c)):
            for t in range(4):
                lo, hi = halves(src[b, :, t * 128:(t + 1) * 128])
                dst[b * 8 + 2 * t] = lo
                dst[b * 8 + 2 * t + 1] = hi

    def relayout(slot, stage):
        for p in range(32):
            v0 = tbuf[pl.ds(pl.multiple_of(slot * 32, 32), 16), p * 128:(p + 1) * 128]
            v1 = tbuf[pl.ds(pl.multiple_of(slot * 32 + 16, 16), 16), p * 128:(p + 1) * 128]
            even = jnp.concatenate([v0[:, :64], v1[:, :64]], axis=1)
            odd = jnp.concatenate([v0[:, 64:], v1[:, 64:]], axis=1)
            stage[pl.ds(32 * p, 16), :] = even.astype(jnp.float32)
            stage[pl.ds(32 * p + 16, 16), :] = odd.astype(jnp.float32)

    def compute(base, stage):
        low = lane_low((16, 128))
        lowu = lane_low((64, 128))
        for s in range(16):
            u = stage[pl.ds(s, 64, stride=16), :].astype(jnp.bfloat16)
            zero = jnp.zeros_like(u)
            bd = jnp.concatenate([jnp.where(lowu, u, zero), jnp.where(lowu, zero, u)], axis=0)
            r0, r1 = rows[base + s], rows[base + 16 + s]
            c0, c1 = cols[base + s], cols[base + 16 + s]
            xc = jnp.where(low, x2c[c0], x2c[c1])
            xr = jnp.where(low, x2r[r0], x2r[r1])
            fo = lax.dot_general(xc, bd, (((1,), (1,)), ((), ())), preferred_element_type=jnp.float32)
            co = lax.dot_general(xr, bd, (((1,), (0,)), ((), ())), preferred_element_type=jnp.float32)
            q = s % copies
            f_acc[2 * q][r0] += fo
            f_acc[2 * q + 1][r1] += fo
            c_acc[2 * q][c0] += co
            c_acc[2 * q + 1][c1] += co

    fetch(0).wait()
    relayout(0, stages[0])

    @pl.loop(0, chunks // 2)
    def _(h):
        for e in range(2):
            k = 2 * h + e
            nxt = jnp.minimum(k + 1, chunks - 1)
            @pl.when(k + 1 < chunks)
            def _():
                fetch(k + 1).wait()
            relayout(nxt, stages[1 - e])
            compute(k * 32, stages[e])

    @pl.loop(0, 16)
    def _(b):
        low = lane_low((16, 128))
        for acc, out in ((f_acc, f_out), (c_acc, c_out)):
            for t in range(4):
                parts = []
                for u in range(2):
                    r = b * 8 + 2 * t + u
                    g0 = acc[0][r]
                    g1 = acc[1][r]
                    for q in range(1, copies):
                        g0 = g0 + acc[2 * q][r]
                        g1 = g1 + acc[2 * q + 1][r]
                    parts.append(g0[:, :64] + g1[:, 64:])
                out[b, :, t * 128:(t + 1) * 128] = jnp.concatenate(parts, axis=1)

def local_products(rows, cols, count, row_set, col_set, tiles, copies=1):
    out = jax.ShapeDtypeStruct((16, 16, 512), jnp.float32)
    smem = pl.BlockSpec(memory_space=pltpu.SMEM)
    vmem = pl.BlockSpec(memory_space=pltpu.VMEM)
    return pl.pallas_call(
        functools.partial(local_kernel, copies),
        out_shape=(out, out),
        in_specs=[smem, smem, smem, vmem, vmem, pl.BlockSpec(memory_space=pl.ANY)],
        out_specs=(vmem, vmem),
        scratch_shapes=[
            pltpu.VMEM((1024, 4096), jnp.bfloat16),
            pltpu.SemaphoreType.DMA((32,)),
            pltpu.VMEM((128, 16, 128), jnp.bfloat16),
            pltpu.VMEM((128, 16, 128), jnp.bfloat16),
            pltpu.VMEM((1024, 128), jnp.float32),
            pltpu.VMEM((1024, 128), jnp.float32),
        ] + [pltpu.VMEM((128, 16, 128), jnp.float32)] * (4 * copies),
        compiler_params=pltpu.CompilerParams(vmem_limit_bytes=60 << 20),
        name="local_products",
    )(rows, cols, count, row_set, col_set, tiles)


def on_device(vectors, tiles, tile_rows, tile_cols, tile_counts):
    row_set, col_set = gather(vectors)
    f, c = local_products(
        tile_rows.reshape(-1), tile_cols.reshape(-1), tile_counts.reshape(-1),
        row_set, col_set, tiles.reshape(tiles.shape[2:]))
    return scatter(f, c)


def solution(mesh):
    return jax.shard_map(
        on_device,
        mesh=mesh,
        in_specs=(
            P(None, ("row", "col")),
            P("row", "col", None, None),
            P("row", "col", None),
            P("row", "col", None),
            P("row", "col"),
        ),
        out_specs=P(None, ("row", "col")),
        check_vma=False,
    )
```

time: 309 us -> 63.1 us (0.20)
  the two profiles are of different devices: /device:TPU:8 before, /device:TPU:6 now
where the time goes in v1:
time: 63.1 us; the launch traced here: 62.9 us
  Pallas kernels  60.8 us (96%)
  local copies, waits for them, and re-layouts  1.38 us (2%)
  between operations  0.68 us (1%)
    pallas_call x1, Pallas kernels, local_products(): pl.pallas_call(functools.partial(local_kernel, copies), out_shape=(out, o...  25.3 us
    pallas_call x1, Pallas kernels, gather(): pl.pallas_call(gather_kernel, out_shape=(whole, whole), in_specs=[vmem],...  19.3 us
    pallas_call x1, Pallas kernels, scatter(): pl.pallas_call(scatter_kernel, out_shape=jax.ShapeDtypeStruct(block, jnp....  16.2 us
    unnamed x1, local copies, waits for them, and re-layouts  1.38 us

profile of v1, /device:TPU:6, one launch (start us, length us, event | category | flops | bytes accessed | tf_op | source)
XLA Modules:
  0.0 62.9 jit_solution(14440059112635037604)
XLA Ops:
  0.7 19.3 %gather.1 = (bf16[16,16,512]{2,1,0:T(8,128)(2,1)}, bf16[16,16,512]{2,1,0:T(8,128)(2,1)}) custom-call(bf16[16,512]{1,0:T(8,128)(2,1)} %vec.1), custom_call_target="tpu_custom_call" | custom-call | tf_op jit(solution)/shard_map/gather/pallas_call | solution.py:107
  20.0 25.3 %local_products.1 = (f32[16,16,512]{2,1,0:T(8,128)}, f32[16,16,512]{2,1,0:T(8,128)}) custom-call(s32[1024]{0:T(1024)} %bitcast.6, s32[1024]{0:T(1024)} %bitcast.7, s32[1]{0:T(128)} %bitcast.4.count, bf16[16,16,512]{2,1,0:T(8,128)(2,1)} %get-tuple-element.9.row_set, bf16[16,16,512]{2,1,0:T(8,128)(2,1)} %get-tuple-element.10.col_set, bf16[1024,4096]{1,0:T(8,128)(2,1)} %bitcast.5), custom_call_target="tpu_custom_call" | custom-call | tf_op jit(solution)/shard_map/local_products/pallas_call | solution.py:300
  45.3 16.2 %scatter.1 = f32[16,512]{1,0:T(8,128)} custom-call(f32[16,16,512]{2,1,0:T(8,128)} %get-tuple-element.11.f, f32[16,16,512]{2,1,0:T(8,128)} %get-tuple-element.12.c), custom_call_target="tpu_custom_call" | custom-call | tf_op jit(solution)/shard_map/scatter/pallas_call | solution.py:184
  61.5 1.4 %copy.8 = f32[16,512]{1,0:T(8,128)} copy(f32[16,512]{1,0:T(8,128)} %scatter.1) | data formatting | bytes 65536

commit v2 on v1

--- a/solution.py
+++ b/solution.py
@@ -114,7 +114,9 @@
             pltpu.SemaphoreType.DMA((16,)),
             pltpu.SemaphoreType.DMA((16,)),
         ],
-        compiler_params=pltpu.CompilerParams(collective_id=0, has_side_effects=True),
+        compiler_params=pltpu.CompilerParams(
+            collective_id=0, has_side_effects=True, vmem_limit_bytes=8 << 20),
+        cost_estimate=pl.CostEstimate(flops=10**10, bytes_accessed=2**22, transcendentals=0),
         name="gather",
     )(vectors)
 
@@ -195,9 +197,14 @@
             pltpu.SemaphoreType.DMA((6,)),
             pltpu.SemaphoreType.DMA,
         ],
-        compiler_params=pltpu.CompilerParams(collective_id=1, has_side_effects=True),
+        compiler_params=pltpu.CompilerParams(
+            collective_id=1, has_side_effects=True, vmem_limit_bytes=8 << 20),
         name="scatter",
     )(f, c)
+
+
+PITCH = 17
+UNROLL = 4
 
 
 def lane_low(shape):
@@ -222,12 +229,12 @@
     def _(k):
         fetch(k).start()
 
-    @pl.loop(0, 128)
+    @pl.loop(0, 128, unroll=8)
     def _(r):
         for acc in f_acc + c_acc:
             acc[r] = jnp.zeros((16, 128), jnp.float32)
 
-    @pl.loop(0, 16)
+    @pl.loop(0, 16, unroll=2)
     def _(b):
         for src, dst in ((row_set, x2r), (col_set, x2c)):
             for t in range(4):
@@ -235,49 +242,72 @@
                 dst[b * 8 + 2 * t] = lo
                 dst[b * 8 + 2 * t + 1] = hi
 
-    def relayout(slot, stage):
-        for p in range(32):
-            v0 = tbuf[pl.ds(pl.multiple_of(slot * 32, 32), 16), p * 128:(p + 1) * 128]
-            v1 = tbuf[pl.ds(pl.multiple_of(slot * 32 + 16, 16), 16), p * 128:(p + 1) * 128]
-            even = jnp.concatenate([v0[:, :64], v1[:, :64]], axis=1)
-            odd = jnp.concatenate([v0[:, 64:], v1[:, 64:]], axis=1)
-            stage[pl.ds(32 * p, 16), :] = even.astype(jnp.float32)
-            stage[pl.ds(32 * p + 16, 16), :] = odd.astype(jnp.float32)
-
-    def compute(base, stage):
-        low = lane_low((16, 128))
-        lowu = lane_low((64, 128))
-        for s in range(16):
-            u = stage[pl.ds(s, 64, stride=16), :].astype(jnp.bfloat16)
-            zero = jnp.zeros_like(u)
-            bd = jnp.concatenate([jnp.where(lowu, u, zero), jnp.where(lowu, zero, u)], axis=0)
-            r0, r1 = rows[base + s], rows[base + 16 + s]
-            c0, c1 = cols[base + s], cols[base + 16 + s]
-            xc = jnp.where(low, x2c[c0], x2c[c1])
-            xr = jnp.where(low, x2r[r0], x2r[r1])
-            fo = lax.dot_general(xc, bd, (((1,), (1,)), ((), ())), preferred_element_type=jnp.float32)
-            co = lax.dot_general(xr, bd, (((1,), (0,)), ((), ())), preferred_element_type=jnp.float32)
-            q = s % copies
-            f_acc[2 * q][r0] += fo
-            f_acc[2 * q + 1][r1] += fo
-            c_acc[2 * q][c0] += co
-            c_acc[2 * q + 1][c1] += co
+    def relayout(k, stage, p):
+        at = pl.multiple_of(k * 32, 32)
+        v0 = tbuf[pl.ds(at, 16), p * 128:(p + 1) * 128]
+        v1 = tbuf[pl.ds(pl.multiple_of(at + 16, 16), 16), p * 128:(p + 1) * 128]
+        even = jnp.concatenate([v0[:, :64], v1[:, :64]], axis=1)
+        odd = jnp.concatenate([v0[:, 64:], v1[:, 64:]], axis=1)
+        stage[pl.ds(PITCH * 2 * p, 16), :] = even.astype(jnp.float32)
+        stage[pl.ds(PITCH * (2 * p + 1), 16), :] = odd.astype(jnp.float32)
+
+    low = lane_low((16, 128))
+    lowu = lane_low((64, 128))
+    nothing = jnp.zeros((16, 128), jnp.bfloat16)
+
+    def blocks(stage, s):
+        u = stage[pl.ds(s, 64, stride=PITCH), :].astype(jnp.bfloat16)
+        zero = jnp.zeros_like(u)
+        return jnp.concatenate([jnp.where(lowu, u, zero), jnp.where(lowu, zero, u)], axis=0)
+
+    def pick(table, i, j):
+        return jnp.where(low, table[i], table[j])
+
+    def two_pairs(base, stage, s):
+        bd = [blocks(stage, s), blocks(stage, s + 1)]
+        r = [(rows[base + s + e], rows[base + 16 + s + e]) for e in (0, 1)]
+        c = [(cols[base + s + e], cols[base + 16 + s + e]) for e in (0, 1)]
+
+        def spread(x):
+            return jnp.concatenate([jnp.concatenate([x[0], nothing], axis=1),
+                                    jnp.concatenate([nothing, x[1]], axis=1)], axis=0)
+
+        xc = spread([pick(x2c, *c[e]) for e in (0, 1)])
+        xr = spread([pick(x2r, *r[e]) for e in (0, 1)])
+        fo = lax.dot_general(xc, jnp.concatenate(bd, axis=1), (((1,), (1,)), ((), ())),
+                             preferred_element_type=jnp.float32)
+        co = lax.dot_general(xr, jnp.concatenate(bd, axis=0), (((1,), (0,)), ((), ())),
+                             preferred_element_type=jnp.float32)
+        for e in (0, 1):
+            q = e % copies
+            f_acc[2 * q][r[e][0]] += fo[16 * e:16 * e + 16]
+            f_acc[2 * q + 1][r[e][1]] += fo[16 * e:16 * e + 16]
+            c_acc[2 * q][c[e][0]] += co[16 * e:16 * e + 16]
+            c_acc[2 * q + 1][c[e][1]] += co[16 * e:16 * e + 16]
 
     fetch(0).wait()
-    relayout(0, stages[0])
-
-    @pl.loop(0, chunks // 2)
+    for p in range(32):
+        relayout(0, stages[0], p)
+
+    @pl.loop(0, chunks // UNROLL)
     def _(h):
-        for e in range(2):
-            k = 2 * h + e
-            nxt = jnp.minimum(k + 1, chunks - 1)
-            @pl.when(k + 1 < chunks)
-            def _():
-                fetch(k + 1).wait()
-            relayout(nxt, stages[1 - e])
-            compute(k * 32, stages[e])
-
-    @pl.loop(0, 16)
+        first = h * UNROLL
+        for e in range(1, UNROLL):
+            fetch(first + e).wait()
+
+        @pl.when(first + UNROLL < chunks)
+        def _():
+            fetch(first + UNROLL).wait()
+
+        for e in range(UNROLL):
+            k = first + e
+            nxt = k + 1 if e < UNROLL - 1 else jnp.minimum(k + 1, chunks - 1)
+            for s in range(0, 16, 2):
+                two_pairs(k * 32, stages[e % 2], s)
+                for p in range(2 * s, 2 * s + 4):
+                    relayout(nxt, stages[1 - e % 2], p)
+
+    @pl.loop(0, 16, unroll=2)
     def _(b):
         low = lane_low((16, 128))
         for acc, out in ((f_acc, f_out), (c_acc, c_out)):
@@ -307,10 +337,10 @@
             pltpu.SemaphoreType.DMA((32,)),
             pltpu.VMEM((128, 16, 128), jnp.bfloat16),
             pltpu.VMEM((128, 16, 128), jnp.bfloat16),
-            pltpu.VMEM((1024, 128), jnp.float32),
-            pltpu.VMEM((1024, 128), jnp.float32),
+            pltpu.VMEM((64 * PITCH, 128), jnp.float32),
+            pltpu.VMEM((64 * PITCH, 128), jnp.float32),
         ] + [pltpu.VMEM((128, 16, 128), jnp.float32)] * (4 * copies),
-        compiler_params=pltpu.CompilerParams(vmem_limit_bytes=60 << 20),
+        compiler_params=pltpu.CompilerParams(vmem_limit_bytes=24 << 20),
         name="local_products",
     )(rows, cols, count, row_set, col_set, tiles)
 

time: 63.1 us -> 47.9 us (0.76)
  the two profiles are of different devices: /device:TPU:6 before, /device:TPU:1 now
where the time goes in v2:
time: 47.9 us; the launch traced here: 47.8 us
  Pallas kernels  45.7 us (95%)
  local copies, waits for them, and re-layouts  1.34 us (3%)
  between operations  0.71 us (1%)
    pallas_call x1, Pallas kernels, scatter(): pl.pallas_call(scatter_kernel, out_shape=jax.ShapeDtypeStruct(block, jnp....  20.2 us
    pallas_call x1, Pallas kernels, gather(): pl.pallas_call(gather_kernel, out_shape=(whole, whole), in_specs=[vmem],...  19.6 us
    pallas_call x1, Pallas kernels, local_products(): pl.pallas_call(functools.partial(local_kernel, copies), out_shape=(out, o...  5.84 us
    unnamed x9, local copies, waits for them, and re-layouts  1.34 us

profile of v2, /device:TPU:1, one launch (start us, length us, event | category | flops | bytes accessed | tf_op | source)
XLA Modules:
  0.0 47.8 jit_solution(14806036652544475479)
XLA Ops:
  0.7 0.0 copy-start.3
  0.7 0.7 %copy-done.3 = bf16[16,512]{1,0:T(8,128)(2,1)S(1)} copy-done((bf16[16,512]{1,0:T(8,128)(2,1)S(1)}, bf16[16,512]{1,0:T(8,128)(2,1)}, u32[]{:S(2)}) %copy-start.3) | copy-done | bytes 16408
  1.4 0.0 copy-start
  1.4 0.0 copy-start.1
  1.4 0.0 copy-start.2
  1.4 19.6 %gather.1 = (bf16[16,16,512]{2,1,0:T(8,128)(2,1)S(1)}, bf16[16,16,512]{2,1,0:T(8,128)(2,1)S(1)}) custom-call(bf16[16,512]{1,0:T(8,128)(2,1)S(1)} %copy-done.3), custom_call_target="tpu_custom_call" | custom-call | flops 10000000000 | bytes 4194304 | tf_op jit(solution)/shard_map/gather/pallas_call | solution.py:107
  21.0 0.0 copy-done
  21.0 0.0 copy-done.1
  21.1 0.0 copy-done.2
  21.1 5.8 %local_products.1 = (f32[16,16,512]{2,1,0:T(8,128)S(1)}, f32[16,16,512]{2,1,0:T(8,128)S(1)}) custom-call(s32[1024]{0:T(1024)S(1)} %bitcast.6, s32[1024]{0:T(1024)S(1)} %bitcast.7, s32[1]{0:T(128)} %bitcast.4.count, bf16[16,16,512]{2,1,0:T(8,128)(2,1)S(1)} %get-tuple-element.9.row_set, bf16[16,16,512]{2,1,0:T(8,128)(2,1)S(1)} %get-tuple-element.10.col_set, ...), custom_call_target="tpu_custom_call" | custom-call | tf_op jit(solution)/shard_map/local_products/pallas_call | solution.py:330
  26.9 20.2 %scatter.1 = f32[16,512]{1,0:T(8,128)S(1)} custom-call(f32[16,16,512]{2,1,0:T(8,128)S(1)} %get-tuple-element.11.f, f32[16,16,512]{2,1,0:T(8,128)S(1)} %get-tuple-element.12.c), custom_call_target="tpu_custom_call" | custom-call | tf_op jit(solution)/shard_map/scatter/pallas_call | solution.py:186
  47.2 0.6 %copy.8 = f32[16,512]{1,0:T(8,128)} copy(f32[16,512]{1,0:T(8,128)S(1)} %scatter.1) | data formatting | bytes 65536
Async XLA Ops:
  0.7 0.7 %copy-start.3 = (bf16[16,512]{1,0:T(8,128)(2,1)S(1)}, bf16[16,512]{1,0:T(8,128)(2,1)}, u32[]{:S(2)}) copy-start(bf16[16,512]{1,0:T(8,128)(2,1)} %vec.1) | copy-start | bytes 49156
  1.4 19.7 %copy-start = (bf16[1,1,1024,4096]{3,2,1,0:T(8,128)(2,1)S(1)}, bf16[1,1,1024,4096]{3,2,1,0:T(8,128)(2,1)}, u32[]{:S(2)}) copy-start(bf16[1,1,1024,4096]{3,2,1,0:T(8,128)(2,1)} %param.6) | copy-start | bytes 25165828
  1.4 19.7 %copy-start.1 = (s32[1,1,1024]{2,1,0:T(1,128)S(1)}, s32[1,1,1024]{2,1,0:T(1,128)}, u32[]{:S(2)}) copy-start(s32[1,1,1024]{2,1,0:T(1,128)} %param.7) | copy-start | bytes 12292
  1.4 19.7 %copy-start.2 = (s32[1,1,1024]{2,1,0:T(1,128)S(1)}, s32[1,1,1024]{2,1,0:T(1,128)}, u32[]{:S(2)}) copy-start(s32[1,1,1024]{2,1,0:T(1,128)} %param.8) | copy-start | bytes 12292

commit v3 on v2

--- a/solution.py
+++ b/solution.py
@@ -22,7 +22,7 @@
     def col(self, dx=0, dz=0):
         return ((self.x + dx) % 4) * 4 + (self.z + dz) % 4
 
-    def meet(self):
+    def greet(self):
         peers = [(self.row(dh=1), self.b), (self.row(dk=1), self.b)]
         peers += [(self.row(dy=d), self.b) for d in (1, 2, 3)]
         peers += [(self.a, self.col(dx=d)) for d in (1, 2, 3)]
@@ -30,7 +30,7 @@
         barrier = pltpu.get_barrier_semaphore()
         for peer in peers:
             pl.semaphore_signal(barrier, inc=1, device_id=peer, device_id_type=MESH)
-        pl.semaphore_wait(barrier, len(peers))
+        return lambda: pl.semaphore_wait(barrier, len(peers))
 
 
 class Sends:
@@ -54,11 +54,23 @@
             copy.wait_send()
 
 
-def gather_kernel(vec, row_set, col_set, send_sems, row_sems, col_sems):
+def halves(v):
+    lo, hi = v[:, :64], v[:, 64:]
+    return jnp.concatenate([lo, lo], axis=1), jnp.concatenate([hi, hi], axis=1)
+
+
+def gather_kernel(vec, x2r, x2c, f_low, f_high, c_low, c_high, row_set, col_set, send_sems, row_sems, col_sems):
     at = Place()
     a, b = at.a, at.b
     sends = Sends(send_sems)
-    at.meet()
+    meet = at.greet()
+
+    @pl.loop(0, 128, unroll=8)
+    def _(r):
+        for acc in (f_low, f_high, c_low, c_high):
+            acc[r] = jnp.zeros((16, 128), jnp.float32)
+
+    meet()
     mine_r, mine_c = row_set.at[b], col_set.at[a]
     sends.go(vec, mine_c, col_sems.at[a], (at.row(dh=1), b))
     for d in (2, 1, 3):
@@ -70,6 +82,15 @@
     sends.go(vec, mine_c, col_sems.at[a], (at.row(dk=1), b))
     row_set[b] = vec[...]
     col_set[a] = vec[...]
+
+    def widen(src, dst, j):
+        for t in range(4):
+            lo, hi = halves(src[j, :, t * 128:(t + 1) * 128])
+            dst[j * 8 + 2 * t] = lo
+            dst[j * 8 + 2 * t + 1] = hi
+
+    widen(row_set, x2r, b)
+    widen(col_set, x2c, a)
 
     def got_r(j):
         sends.arrived(row_set.at[j], row_sems.at[j], (a, b))
@@ -92,24 +113,36 @@
             j = at.row(dy=d, dh=dh)
             got_c(j)
             sends.go(col_set.at[j], col_set.at[j], col_sems.at[j], (at.row(dk=1), b))
+    for d in (1, 2, 3):
+        widen(row_set, x2r, at.col(dz=d))
+        widen(col_set, x2c, at.row(dy=d))
+    for d in (0, 1, 2, 3):
+        widen(col_set, x2c, at.row(dy=d, dh=1))
     for dh in (0, 1):
         for d in (0, 1, 2, 3):
-            got_c(at.row(dy=d, dh=dh, dk=1))
+            j = at.row(dy=d, dh=dh, dk=1)
+            got_c(j)
+            widen(col_set, x2c, j)
     for d in (1, 3, 2):
         for e in (0, 1, 3, 2):
-            got_r(at.col(dx=d, dz=e))
+            j = at.col(dx=d, dz=e)
+            got_r(j)
+            widen(row_set, x2r, j)
     sends.finish()
 
 
 def gather(vectors):
-    whole = jax.ShapeDtypeStruct((16,) + vectors.shape, vectors.dtype)
+    whole = pltpu.VMEM((16,) + vectors.shape, vectors.dtype)
+    table = jax.ShapeDtypeStruct((128, 16, 128), vectors.dtype)
+    sums = jax.ShapeDtypeStruct((128, 16, 128), jnp.float32)
     vmem = pl.BlockSpec(memory_space=pltpu.VMEM)
     return pl.pallas_call(
         gather_kernel,
-        out_shape=(whole, whole),
+        out_shape=(table,) * 2 + (sums,) * 4,
         in_specs=[vmem],
-        out_specs=(vmem, vmem),
+        out_specs=(vmem,) * 6,
         scratch_shapes=[
+            whole, whole,
             pltpu.SemaphoreType.DMA((30,)),
             pltpu.SemaphoreType.DMA((16,)),
             pltpu.SemaphoreType.DMA((16,)),
@@ -121,20 +154,53 @@
     )(vectors)
 
 
-def scatter_kernel(f, c, out, fx, fs, fz, cc, cs, cy, ch, send_sems, fx_sems, fz_sems, cc_sems, cy_sems, ch_sem):
+def scatter_kernel(f_low, f_high, c_low, c_high, out, f, c, fx, fs, fz, cc, cs, cy, ch,
+                   send_sems, fx_sems, fz_sems, cc_sems, cy_sems, ch_sem):
     at = Place()
     a, b = at.a, at.b
     sends = Sends(send_sems)
-    at.meet()
+    meet = at.greet()
     far = (2, 1, 3)
-    for dy in (2, 1, 3, 0):
+
+    def emit(low, high, whole, j):
+        for t in range(4):
+            parts = [low[j * 8 + 2 * t + u, :, :64] + high[j * 8 + 2 * t + u, :, 64:] for u in (0, 1)]
+            whole[j, :, t * 128:(t + 1) * 128] = jnp.concatenate(parts, axis=1)
+
+    def emit_f(j):
+        emit(f_low, f_high, f, j)
+
+    def emit_c(j):
+        emit(c_low, c_high, c, j)
+
+    def send_f(dz):
+        for dx in far:
+            n = dz * 3 + dx - 1
+            j = at.col(dx=dx, dz=dz)
+            if dz != 2:
+                emit_f(j)
+            sends.go(f.at[j], fx.at[n], fx_sems.at[n], (a, at.col(dx=dx)))
+
+    def send_c(dy):
         for dh in (1, 0):
             n = dy * 2 + dh
-            sends.go(c.at[at.row(dy=dy, dh=dh, dk=1)], cc.at[n], cc_sems.at[n], (at.row(dk=1), b))
-    for dz in (2, 1, 3, 0):
-        for dx in far:
-            n = dz * 3 + dx - 1
-            sends.go(f.at[at.col(dx=dx, dz=dz)], fx.at[n], fx_sems.at[n], (a, at.col(dx=dx)))
+            j = at.row(dy=dy, dh=dh, dk=1)
+            if dy != 2:
+                emit_c(j)
+            sends.go(c.at[j], cc.at[n], cc_sems.at[n], (at.row(dk=1), b))
+
+    for dx in far:
+        emit_f(at.col(dx=dx, dz=2))
+    for dh in (1, 0):
+        emit_c(at.row(dy=2, dh=dh, dk=1))
+    meet()
+    for d in (2, 1, 3, 0):
+        send_f(d)
+        send_c(d)
+    for d in (2, 1, 3, 0):
+        emit_f(at.col(dz=d))
+        for dh in (1, 0):
+            emit_c(at.row(dy=d, dh=dh))
 
     def sum_core(dy, dh):
         n = dy * 2 + dh
@@ -176,8 +242,7 @@
     sends.finish()
 
 
-def scatter(f, c):
-    block = f.shape[1:]
+def scatter(block, sums):
     vmem = pl.BlockSpec(memory_space=pltpu.VMEM)
 
     def room(n):
@@ -186,10 +251,10 @@
     return pl.pallas_call(
         scatter_kernel,
         out_shape=jax.ShapeDtypeStruct(block, jnp.float32),
-        in_specs=[vmem, vmem],
+        in_specs=[vmem] * 4,
         out_specs=vmem,
         scratch_shapes=[
-            room(12), room(4), room(3), room(8), room(8), room(6), pltpu.VMEM(block, jnp.float32),
+            room(16), room(16), room(12), room(4), room(3), room(8), room(8), room(6), pltpu.VMEM(block, jnp.float32),
             pltpu.SemaphoreType.DMA((30,)),
             pltpu.SemaphoreType.DMA((12,)),
             pltpu.SemaphoreType.DMA((3,)),
@@ -200,7 +265,7 @@
         compiler_params=pltpu.CompilerParams(
             collective_id=1, has_side_effects=True, vmem_limit_bytes=8 << 20),
         name="scatter",
-    )(f, c)
+    )(*sums)
 
 
 PITCH = 17
@@ -210,42 +275,15 @@
 def lane_low(shape):
     return lax.broadcasted_iota(jnp.int32, shape, 1) < 64
 
-def halves(v):
-    lo, hi = v[:, :64], v[:, 64:]
-    return jnp.concatenate([lo, lo], axis=1), jnp.concatenate([hi, hi], axis=1)
-
-def local_kernel(copies, rows, cols, count, row_set, col_set, tiles, f_out, c_out, *scratch):
-    tbuf, tsem, x2r, x2c = scratch[:4]
-    stages = scratch[4:6]
-    f_acc = scratch[6:6 + 2 * copies]
-    c_acc = scratch[6 + 2 * copies:6 + 4 * copies]
+
+def local_kernel(rows, cols, count, x2r, x2c, tiles, f0, f1, c0, c1, f_low, f_high, c_low, c_high, *stages):
+    f_acc, c_acc = (f_low, f_high), (c_low, c_high)
     chunks = count[0] // 32
-
-    def fetch(k):
-        at = pl.ds(pl.multiple_of(k * 32, 32), 32)
-        return pltpu.make_async_copy(tiles.at[at, :], tbuf.at[at, :], tsem.at[k])
-
-    @pl.loop(0, chunks)
-    def _(k):
-        fetch(k).start()
-
-    @pl.loop(0, 128, unroll=8)
-    def _(r):
-        for acc in f_acc + c_acc:
-            acc[r] = jnp.zeros((16, 128), jnp.float32)
-
-    @pl.loop(0, 16, unroll=2)
-    def _(b):
-        for src, dst in ((row_set, x2r), (col_set, x2c)):
-            for t in range(4):
-                lo, hi = halves(src[b, :, t * 128:(t + 1) * 128])
-                dst[b * 8 + 2 * t] = lo
-                dst[b * 8 + 2 * t + 1] = hi
 
     def relayout(k, stage, p):
         at = pl.multiple_of(k * 32, 32)
-        v0 = tbuf[pl.ds(at, 16), p * 128:(p + 1) * 128]
-        v1 = tbuf[pl.ds(pl.multiple_of(at + 16, 16), 16), p * 128:(p + 1) * 128]
+        v0 = tiles[pl.ds(at, 16), p * 128:(p + 1) * 128]
+        v1 = tiles[pl.ds(pl.multiple_of(at + 16, 16), 16), p * 128:(p + 1) * 128]
         even = jnp.concatenate([v0[:, :64], v1[:, :64]], axis=1)
         odd = jnp.concatenate([v0[:, 64:], v1[:, 64:]], axis=1)
         stage[pl.ds(PITCH * 2 * p, 16), :] = even.astype(jnp.float32)
@@ -279,26 +317,17 @@
         co = lax.dot_general(xr, jnp.concatenate(bd, axis=0), (((1,), (0,)), ((), ())),
                              preferred_element_type=jnp.float32)
         for e in (0, 1):
-            q = e % copies
-            f_acc[2 * q][r[e][0]] += fo[16 * e:16 * e + 16]
-            f_acc[2 * q + 1][r[e][1]] += fo[16 * e:16 * e + 16]
-            c_acc[2 * q][c[e][0]] += co[16 * e:16 * e + 16]
-            c_acc[2 * q + 1][c[e][1]] += co[16 * e:16 * e + 16]
-
-    fetch(0).wait()
+            f_acc[0][r[e][0]] += fo[16 * e:16 * e + 16]
+            f_acc[1][r[e][1]] += fo[16 * e:16 * e + 16]
+            c_acc[0][c[e][0]] += co[16 * e:16 * e + 16]
+            c_acc[1][c[e][1]] += co[16 * e:16 * e + 16]
+
     for p in range(32):
         relayout(0, stages[0], p)
 
     @pl.loop(0, chunks // UNROLL)
     def _(h):
         first = h * UNROLL
-        for e in range(1, UNROLL):
-            fetch(first + e).wait()
-
-        @pl.when(first + UNROLL < chunks)
-        def _():
-            fetch(first + UNROLL).wait()
-
         for e in range(UNROLL):
             k = first + e
             nxt = k + 1 if e < UNROLL - 1 else jnp.minimum(k + 1, chunks - 1)
@@ -307,50 +336,28 @@
                 for p in range(2 * s, 2 * s + 4):
                     relayout(nxt, stages[1 - e % 2], p)
 
-    @pl.loop(0, 16, unroll=2)
-    def _(b):
-        low = lane_low((16, 128))
-        for acc, out in ((f_acc, f_out), (c_acc, c_out)):
-            for t in range(4):
-                parts = []
-                for u in range(2):
-                    r = b * 8 + 2 * t + u
-                    g0 = acc[0][r]
-                    g1 = acc[1][r]
-                    for q in range(1, copies):
-                        g0 = g0 + acc[2 * q][r]
-                        g1 = g1 + acc[2 * q + 1][r]
-                    parts.append(g0[:, :64] + g1[:, 64:])
-                out[b, :, t * 128:(t + 1) * 128] = jnp.concatenate(parts, axis=1)
-
-def local_products(rows, cols, count, row_set, col_set, tiles, copies=1):
-    out = jax.ShapeDtypeStruct((16, 16, 512), jnp.float32)
+
+def local_products(rows, cols, count, x2r, x2c, tiles, sums):
     smem = pl.BlockSpec(memory_space=pltpu.SMEM)
     vmem = pl.BlockSpec(memory_space=pltpu.VMEM)
     return pl.pallas_call(
-        functools.partial(local_kernel, copies),
-        out_shape=(out, out),
-        in_specs=[smem, smem, smem, vmem, vmem, pl.BlockSpec(memory_space=pl.ANY)],
-        out_specs=(vmem, vmem),
-        scratch_shapes=[
-            pltpu.VMEM((1024, 4096), jnp.bfloat16),
-            pltpu.SemaphoreType.DMA((32,)),
-            pltpu.VMEM((128, 16, 128), jnp.bfloat16),
-            pltpu.VMEM((128, 16, 128), jnp.bfloat16),
-            pltpu.VMEM((64 * PITCH, 128), jnp.float32),
-            pltpu.VMEM((64 * PITCH, 128), jnp.float32),
-        ] + [pltpu.VMEM((128, 16, 128), jnp.float32)] * (4 * copies),
+        local_kernel,
+        out_shape=tuple(jax.ShapeDtypeStruct(v.shape, v.dtype) for v in sums),
+        in_specs=[smem] * 3 + [vmem] * 7,
+        out_specs=(vmem,) * 4,
+        input_output_aliases={6: 0, 7: 1, 8: 2, 9: 3},
+        scratch_shapes=[pltpu.VMEM((64 * PITCH, 128), jnp.float32)] * 2,
         compiler_params=pltpu.CompilerParams(vmem_limit_bytes=24 << 20),
         name="local_products",
-    )(rows, cols, count, row_set, col_set, tiles)
+    )(rows, cols, count, x2r, x2c, tiles, *sums)
 
 
 def on_device(vectors, tiles, tile_rows, tile_cols, tile_counts):
-    row_set, col_set = gather(vectors)
-    f, c = local_products(
+    x2r, x2c, *sums = gather(vectors)
+    sums = local_products(
         tile_rows.reshape(-1), tile_cols.reshape(-1), tile_counts.reshape(-1),
-        row_set, col_set, tiles.reshape(tiles.shape[2:]))
-    return scatter(f, c)
+        x2r, x2c, tiles.reshape(tiles.shape[2:]), sums)
+    return scatter(vectors.shape, sums)
 
 
 def solution(mesh):

time: 47.9 us -> 45.7 us (0.954)
  Pallas kernels: 45.7 us -> 43.2 us
    pallas_call x1, Pallas kernels: 20.2 us -> 17.7 us  [scatter(): pl.pallas_call(scatter_kernel, out_shape=jax.ShapeDtypeStruct(block, jnp....]
where the time goes in v3:
time: 45.7 us; the launch traced here: 45.2 us
  Pallas kernels  43.2 us (95%)
  local copies, waits for them, and re-layouts  1.34 us (3%)
  between operations  0.71 us (2%)
    pallas_call x1, Pallas kernels, gather(): pl.pallas_call(gather_kernel, out_shape=(table,) * 2 + (sums,) * 4, in_sp...  20.7 us
    pallas_call x1, Pallas kernels, scatter(): pl.pallas_call(scatter_kernel, out_shape=jax.ShapeDtypeStruct(block, jnp....  17.7 us
    pallas_call x1, Pallas kernels, local_products(): pl.pallas_call(local_kernel, out_shape=tuple((jax.ShapeDtypeStruct(v.shap...  4.85 us
    unnamed x9, local copies, waits for them, and re-layouts  1.34 us

profile of v3, /device:TPU:1, one launch (start us, length us, event | category | flops | bytes accessed | tf_op | source)
XLA Modules:
  0.0 45.2 jit_solution(9505510165599270193)
XLA Ops:
  0.7 0.0 copy-start.3
  0.7 0.7 %copy-done.3 = bf16[16,512]{1,0:T(8,128)(2,1)S(1)} copy-done((bf16[16,512]{1,0:T(8,128)(2,1)S(1)}, bf16[16,512]{1,0:T(8,128)(2,1)}, u32[]{:S(2)}) %copy-start.3) | copy-done | bytes 16408
  1.4 0.0 copy-start
  1.4 0.0 copy-start.1
  1.4 0.0 copy-start.2
  1.4 20.7 %gather.1 = (bf16[128,16,128]{2,1,0:T(8,128)(2,1)S(1)}, bf16[128,16,128]{2,1,0:T(8,128)(2,1)S(1)}, f32[128,16,128]{2,1,0:T(8,128)S(1)}, f32[128,16,128]{2,1,0:T(...) custom-call(bf16[16,512]{1,0:T(8,128)(2,1)S(1)} %copy-done.3), custom_call_target="tpu_custom_call" | custom-call | flops 10000000000 | bytes 4194304 | tf_op jit(solution)/shard_map/gather/pallas_call | solution.py:139
  22.1 0.0 copy-done
  22.1 0.0 copy-done.1
  22.1 0.0 copy-done.2
  22.1 4.8 %local_products.1 = (f32[128,16,128]{2,1,0:T(8,128)S(1)}, f32[128,16,128]{2,1,0:T(8,128)S(1)}, f32[128,16,128]{2,1,0:T(8,128)S(1)}, f32[128,16,128]{2,1,0:T(8,128)S(1)}) custom-call(s32[1024]{0:T(1024)S(1)} %bitcast.6, s32[1024]{0:T(1024)S(1)} %bitcast.7, s32[1]{0:T(128)} %bitcast.4.count, ...), custom_call_target="tpu_custom_call", output_to_operand_aliasing={{0}: (6, {}), {1}: (7, {}), {2}: (8, {}), {3}: (9, {})} | custom-call | tf_op jit(solution)/shard_map/local_products/pallas_call | solution.py:343
  26.9 17.7 %scatter.1 = f32[16,512]{1,0:T(8,128)S(1)} custom-call(f32[128,16,128]{2,1,0:T(8,128)S(1)} %get-tuple-element.21.f_low, f32[128,16,128]{2,1,0:T(8,128)S(1)} %get-tuple-element.22.f_high, f32[128,16,128]{2,1,0:T(8,128)S(1)} %get-tuple-element.23.c_low, f32[128,16,128]{2,1,0:T(8,128)S(1)} %get-tuple-element.24.c_high), custom_call_target="tpu_custom_call" | custom-call | tf_op jit(solution)/shard_map/scatter/pallas_call | solution.py:251
  44.6 0.6 %copy.16 = f32[16,512]{1,0:T(8,128)} copy(f32[16,512]{1,0:T(8,128)S(1)} %scatter.1) | data formatting | bytes 65536
Async XLA Ops:
  0.7 0.7 %copy-start.3 = (bf16[16,512]{1,0:T(8,128)(2,1)S(1)}, bf16[16,512]{1,0:T(8,128)(2,1)}, u32[]{:S(2)}) copy-start(bf16[16,512]{1,0:T(8,128)(2,1)} %vec.1) | copy-start | bytes 49156
  1.4 20.7 %copy-start = (bf16[1,1,1024,4096]{3,2,1,0:T(8,128)(2,1)S(1)}, bf16[1,1,1024,4096]{3,2,1,0:T(8,128)(2,1)}, u32[]{:S(2)}) copy-start(bf16[1,1,1024,4096]{3,2,1,0:T(8,128)(2,1)} %param.6) | copy-start | bytes 25165828
  1.4 20.7 %copy-start.1 = (s32[1,1,1024]{2,1,0:T(1,128)S(1)}, s32[1,1,1024]{2,1,0:T(1,128)}, u32[]{:S(2)}) copy-start(s32[1,1,1024]{2,1,0:T(1,128)} %param.7) | copy-start | bytes 12292
  1.4 20.7 %copy-start.2 = (s32[1,1,1024]{2,1,0:T(1,128)S(1)}, s32[1,1,1024]{2,1,0:T(1,128)}, u32[]{:S(2)}) copy-start(s32[1,1,1024]{2,1,0:T(1,128)} %param.8) | copy-start | bytes 12292

commit v4 on v3

--- a/solution.py
+++ b/solution.py
@@ -59,29 +59,33 @@
     return jnp.concatenate([lo, lo], axis=1), jnp.concatenate([hi, hi], axis=1)
 
 
-def gather_kernel(vec, x2r, x2c, f_low, f_high, c_low, c_high, row_set, col_set, send_sems, row_sems, col_sems):
+def gather_kernel(vec, x2r, x2c, f_low, f_high, c_low, c_high, row_set, col_set, own_sems, send_sems, row_sems, col_sems):
     at = Place()
     a, b = at.a, at.b
     sends = Sends(send_sems)
     meet = at.greet()
+    own = [pltpu.make_async_copy(vec, row_set.at[b], own_sems.at[0]),
+           pltpu.make_async_copy(vec, col_set.at[a], own_sems.at[1])]
+    for copy in own:
+        copy.start()
 
     @pl.loop(0, 128, unroll=8)
     def _(r):
         for acc in (f_low, f_high, c_low, c_high):
             acc[r] = jnp.zeros((16, 128), jnp.float32)
 
+    for copy in own:
+        copy.wait()
     meet()
     mine_r, mine_c = row_set.at[b], col_set.at[a]
-    sends.go(vec, mine_c, col_sems.at[a], (at.row(dh=1), b))
+    sends.go(mine_c, mine_c, col_sems.at[a], (at.row(dh=1), b))
     for d in (2, 1, 3):
-        sends.go(vec, mine_r, row_sems.at[b], (a, at.col(dz=d)))
+        sends.go(mine_r, mine_r, row_sems.at[b], (a, at.col(dz=d)))
     for d in (2, 1, 3):
-        sends.go(vec, mine_c, col_sems.at[a], (at.row(dy=d), b))
+        sends.go(mine_c, mine_c, col_sems.at[a], (at.row(dy=d), b))
     for d in (2, 1, 3):
-        sends.go(vec, mine_r, row_sems.at[b], (a, at.col(dx=d)))
-    sends.go(vec, mine_c, col_sems.at[a], (at.row(dk=1), b))
-    row_set[b] = vec[...]
-    col_set[a] = vec[...]
+        sends.go(mine_r, mine_r, row_sems.at[b], (a, at.col(dx=d)))
+    sends.go(mine_c, mine_c, col_sems.at[a], (at.row(dk=1), b))
 
     def widen(src, dst, j):
         for t in range(4):
@@ -139,10 +143,11 @@
     return pl.pallas_call(
         gather_kernel,
         out_shape=(table,) * 2 + (sums,) * 4,
-        in_specs=[vmem],
+        in_specs=[pl.BlockSpec(memory_space=pltpu.HBM)],
         out_specs=(vmem,) * 6,
         scratch_shapes=[
             whole, whole,
+            pltpu.SemaphoreType.DMA((2,)),
             pltpu.SemaphoreType.DMA((30,)),
             pltpu.SemaphoreType.DMA((16,)),
             pltpu.SemaphoreType.DMA((16,)),
@@ -353,7 +358,7 @@
 
 
 def on_device(vectors, tiles, tile_rows, tile_cols, tile_counts):
-    x2r, x2c, *sums = gather(vectors)
+    x2r, x2c, *sums = gather(pltpu.with_memory_space_constraint(vectors, pltpu.HBM))
     sums = local_products(
         tile_rows.reshape(-1), tile_cols.reshape(-1), tile_counts.reshape(-1),
         x2r, x2c, tiles.reshape(tiles.shape[2:]), sums)

time: 45.7 us -> 45.5 us (level)
  local copies, waits for them, and re-layouts: 1.34 us -> 0.63 us
    pallas_call x1, Pallas kernels: 4.85 us -> 1.81 us  [local_products(): pl.pallas_call(local_kernel, out_shape=tuple((jax.ShapeDtypeStruct(v.shap...]
    pallas_call x1, Pallas kernels: 17.7 us -> 20.6 us  [scatter(): pl.pallas_call(scatter_kernel, out_shape=jax.ShapeDtypeStruct(block, jnp....]
    unnamed x9 -> x7, local copies, waits for them, and re-layouts: 1.34 us -> 0.63 us
where the time goes in v4:
time: 45.5 us; the launch traced here: 44.7 us
  Pallas kernels  43.3 us (95%)
  between operations  0.72 us (2%)
  local copies, waits for them, and re-layouts  0.63 us (1%)
    pallas_call x1, Pallas kernels, gather(): pl.pallas_call(gather_kernel, out_shape=(table,) * 2 + (sums,) * 4, in_sp...  20.9 us
    pallas_call x1, Pallas kernels, scatter(): pl.pallas_call(scatter_kernel, out_shape=jax.ShapeDtypeStruct(block, jnp....  20.6 us
    pallas_call x1, Pallas kernels, local_products(): pl.pallas_call(local_kernel, out_shape=tuple((jax.ShapeDtypeStruct(v.shap...  1.81 us

profile of v4, /device:TPU:1, one launch (start us, length us, event | category | flops | bytes accessed | tf_op | source)
XLA Modules:
  0.0 44.7 jit_solution(16879118498957802820)
XLA Ops:
  0.7 0.0 copy-start
  0.7 0.0 copy-start.1
  0.7 0.0 copy-start.2
  0.7 20.9 %gather.1 = (bf16[128,16,128]{2,1,0:T(8,128)(2,1)S(1)}, bf16[128,16,128]{2,1,0:T(8,128)(2,1)S(1)}, f32[128,16,128]{2,1,0:T(8,128)S(1)}, f32[128,16,128]{2,1,0:T(...) custom-call(bf16[16,512]{1,0:T(8,128)(2,1)} %vec.1), custom_call_target="tpu_custom_call" | custom-call | flops 10000000000 | bytes 4194304 | tf_op jit(solution)/shard_map/gather/pallas_call | solution.py:143
  21.6 0.0 copy-done
  21.6 0.0 copy-done.1
  21.6 0.0 copy-done.2
  21.6 1.8 %local_products.1 = (f32[128,16,128]{2,1,0:T(8,128)S(1)}, f32[128,16,128]{2,1,0:T(8,128)S(1)}, f32[128,16,128]{2,1,0:T(8,128)S(1)}, f32[128,16,128]{2,1,0:T(8,128)S(1)}) custom-call(s32[1024]{0:T(1024)S(1)} %bitcast.6, s32[1024]{0:T(1024)S(1)} %bitcast.7, s32[1]{0:T(128)} %bitcast.4.count, ...), custom_call_target="tpu_custom_call", output_to_operand_aliasing={{0}: (6, {}), {1}: (7, {}), {2}: (8, {}), {3}: (9, {})} | custom-call | tf_op jit(solution)/shard_map/local_products/pallas_call | solution.py:348
  23.5 20.6 %scatter.1 = f32[16,512]{1,0:T(8,128)S(1)} custom-call(f32[128,16,128]{2,1,0:T(8,128)S(1)} %get-tuple-element.21.f_low, f32[128,16,128]{2,1,0:T(8,128)S(1)} %get-tuple-element.22.f_high, f32[128,16,128]{2,1,0:T(8,128)S(1)} %get-tuple-element.23.c_low, f32[128,16,128]{2,1,0:T(8,128)S(1)} %get-tuple-element.24.c_high), custom_call_target="tpu_custom_call" | custom-call | tf_op jit(solution)/shard_map/scatter/pallas_call | solution.py:256
  44.1 0.6 %copy.16 = f32[16,512]{1,0:T(8,128)} copy(f32[16,512]{1,0:T(8,128)S(1)} %scatter.1) | data formatting | bytes 65536
Async XLA Ops:
  0.7 21.0 %copy-start = (bf16[1,1,1024,4096]{3,2,1,0:T(8,128)(2,1)S(1)}, bf16[1,1,1024,4096]{3,2,1,0:T(8,128)(2,1)}, u32[]{:S(2)}) copy-start(bf16[1,1,1024,4096]{3,2,1,0:T(8,128)(2,1)} %param.6) | copy-start | bytes 25165828
  0.7 21.0 %copy-start.1 = (s32[1,1,1024]{2,1,0:T(1,128)S(1)}, s32[1,1,1024]{2,1,0:T(1,128)}, u32[]{:S(2)}) copy-start(s32[1,1,1024]{2,1,0:T(1,128)} %param.7) | copy-start | bytes 12292
  0.7 21.0 %copy-start.2 = (s32[1,1,1024]{2,1,0:T(1,128)S(1)}, s32[1,1,1024]{2,1,0:T(1,128)}, u32[]{:S(2)}) copy-start(s32[1,1,1024]{2,1,0:T(1,128)} %param.8) | copy-start | bytes 12292
